TPU v7x, 256 devices: a whole 4x4x8 slice. The times are simulated.
256 devices in a mesh: section: 4 (over x), dp: 64 (over y, z, core).
Axes of the slice: x: 4, y: 4, z: 8, core: 2. Of those that a mesh axis runs over, the one named last changes fastest.
Arguments:
- clean_latent: bfloat16 [8192, 1536], P('dp'), may hold values from -60 to 60
- noise_latent: bfloat16 [8192, 1536], P('dp'), may hold values from -6 to 6
- teacher_velocity: bfloat16 [8192, 1536], P('dp'), may hold values from -6 to 6
- step_index: int32 [8192], P('dp'), may hold values from 0 to 3
- modulation: float32 [4, 4, 1536], P('section'), may hold values from -0.6 to 0.6
- up_weight: bfloat16 [4, 36864, 128], P('section', 'dp'), may hold values from -0.21875 to 0.21875
- up_rows: int32 [4, 48, 6], P('section'), may hold values from 0 to 11, as said below
- down_weight: bfloat16 [4, 36864, 128], P('section'), may hold values from -0.109375 to 0.109375
- down_rows: int32 [4, 12, 24], P('section'), may hold values from 0 to 47, as said below
Outputs:
- grad_down: float32 [4, 36864, 128], P('section', 'dp')
Inputs may be any that keep to these rules, and one draw needn't show every extreme that they name: For every section s and hidden block c, up_rows[s, c] holds 6 different feature blocks. For every section s and feature block e, down_rows[s, e] holds 24 different hidden blocks.
All inputs are finite; a program needn't handle non-finite values.
Results may differ from a plain program's by a relative error of at most 0.004.
Values may be sent and summed in bfloat16 or wider, within the bound.
No kernel may reach another device: no remote copies, remote signals or barrier semaphores. Data moves between devices by JAX's collectives and lax.ppermute only.
A program may use at most 128 MiB of HBM per device.

v0:
```python
import math
import jax
import jax.numpy as jnp
from jax import lax
from jax.sharding import PartitionSpec as P

MICRO = 2
EPSILON = 1e-06


def from_behind(block, axis, distance):
    devices = range(lax.axis_size(axis))
    route = [(i - distance, i) for i in devices if i - distance in devices]
    return lax.ppermute(block, axis, route)


def activation(values):
    return jax.nn.gelu(values, approximate=True)


def lookup(step_values, table):
    onehot = (step_values[:, None] == jnp.arange(table.shape[0], dtype=jnp.int32)[None, :]).astype(
        jnp.float32
    )
    return jnp.sum(onehot[:, :, None] * table[None, :, :], axis=1)


def section_forward(stream, scale_rows, up_blocks, up_index, down_blocks, down_index):
    row_count, feature_count = stream.shape
    block_size = up_blocks.shape[-1]
    stream_wide = stream.astype(jnp.float32)
    inverse = lax.rsqrt(jnp.mean(stream_wide * stream_wide, axis=-1, keepdims=True) + EPSILON)
    normed = (stream_wide * inverse * (1.0 + scale_rows)).astype(jnp.bfloat16)
    picked = normed.reshape(row_count, feature_count // block_size, block_size)[:, up_index, :]
    preact = jnp.einsum("rcki,ckij->rcj", picked, up_blocks, preferred_element_type=jnp.float32)
    hidden = activation(preact).astype(jnp.bfloat16)
    gathered = hidden[:, down_index, :]
    mixed_out = jnp.einsum(
        "rekj,ekjf->ref", gathered, down_blocks, preferred_element_type=jnp.float32
    )
    result = (stream_wide + mixed_out.reshape(row_count, feature_count)).astype(jnp.bfloat16)
    return (result, preact.reshape(row_count, -1), hidden.reshape(row_count, -1))


def section_backward(
    cotangent, stream, scale_rows, preact, up_blocks, up_index, down_blocks, down_index
):
    row_count, feature_count = stream.shape
    block_size = up_blocks.shape[-1]
    hidden_count = preact.shape[1]
    grad_blocks = cotangent.reshape(row_count, feature_count // block_size, block_size)
    grad_gathered = jnp.einsum(
        "ref,ekjf->rekj", grad_blocks, down_blocks, preferred_element_type=jnp.float32
    )
    grad_hidden = (
        jnp.zeros((row_count, hidden_count // block_size, block_size), jnp.float32)
        .at[:, down_index, :]
        .add(grad_gathered)
    )
    activated, pullback = jax.vjp(
        activation, preact.reshape(row_count, hidden_count // block_size, block_size)
    )
    grad_preact = pullback(grad_hidden)[0].astype(jnp.bfloat16)
    grad_picked = jnp.einsum(
        "rcj,ckij->rcki", grad_preact, up_blocks, preferred_element_type=jnp.float32
    )
    grad_normed = (
        jnp.zeros((row_count, feature_count // block_size, block_size), jnp.float32)
        .at[:, up_index, :]
        .add(grad_picked)
    )
    grad_normed = grad_normed.reshape(row_count, feature_count)
    stream_wide = stream.astype(jnp.float32)
    inverse = lax.rsqrt(jnp.mean(stream_wide * stream_wide, axis=-1, keepdims=True) + EPSILON)
    scaled = grad_normed * (1.0 + scale_rows)
    grad_stream = inverse * scaled - stream_wide * inverse * inverse * inverse * jnp.mean(
        scaled * stream_wide, axis=-1, keepdims=True
    )
    return (cotangent.astype(jnp.float32) + grad_stream).astype(jnp.bfloat16)


def pick_slot(stack, index):
    return lax.dynamic_index_in_dim(stack, index, 0, keepdims=False)


def store_slot(stack, index, value, valid):
    previous = pick_slot(stack, index)
    return lax.dynamic_update_index_in_dim(stack, jnp.where(valid, value, previous), index, 0)


def per_device(
    clean_latent,
    noise_latent,
    teacher_velocity,
    step_index,
    modulation,
    up_weight,
    up_rows,
    down_weight,
    down_rows,
):
    section_count = lax.axis_size("section")
    section_number = lax.axis_index("section")
    owner_count = lax.axis_size("dp")
    row_total, feature_count = clean_latent.shape
    block_size = up_weight.shape[2]
    hidden_blocks, keep_up = (up_rows.shape[1], up_rows.shape[2])
    width_blocks, keep_down = (down_rows.shape[1], down_rows.shape[2])
    hidden_count = hidden_blocks * block_size
    micro_rows = row_total // MICRO
    turn_count = MICRO + section_count - 1
    loss_scale = 1.0 / math.sqrt(row_total * owner_count)
    gathered_up = lax.all_gather(up_weight, "dp", axis=1, tiled=True)
    up_blocks = gathered_up.reshape(hidden_blocks, keep_up, block_size, block_size)
    up_index = up_rows[0]
    down_blocks = down_weight.reshape(width_blocks, keep_down, block_size, block_size)
    down_index = down_rows[0]
    table = modulation[0]
    fraction = (step_index.astype(jnp.float32) + 1.0) / table.shape[0]
    entry = (
        (1.0 - fraction)[:, None] * clean_latent.astype(jnp.float32)
        + fraction[:, None] * noise_latent.astype(jnp.float32)
    ).astype(jnp.bfloat16)
    entry = entry.reshape(MICRO, micro_rows, feature_count)
    scale_all = lookup(step_index, table).reshape(MICRO, micro_rows, feature_count)
    targets = teacher_velocity.reshape(MICRO, micro_rows, feature_count)

    def forward_turn(turn_index, carry):
        arrived, kept_stream, kept_preact, kept_hidden, kept_grad = carry
        micro_index = turn_index - section_number
        valid = (micro_index >= 0) & (micro_index < MICRO)
        clipped = jnp.clip(micro_index, 0, MICRO - 1)
        stream_in = jnp.where(section_number == 0, pick_slot(entry, clipped), arrived)
        scale_rows = pick_slot(scale_all, clipped)

        def forward_active(operand):
            return section_forward(
                stream_in, scale_rows, up_blocks, up_index, down_blocks, down_index
            )

        def forward_resting(operand):
            return (
                jnp.zeros_like(stream_in),
                jnp.zeros((micro_rows, hidden_count), jnp.float32),
                jnp.zeros((micro_rows, hidden_count), jnp.bfloat16),
            )

        result, preact, hidden = lax.cond(valid, forward_active, forward_resting, 0)
        cotangent = (
            (result.astype(jnp.float32) - pick_slot(targets, clipped).astype(jnp.float32))
            * loss_scale
        ).astype(jnp.bfloat16)
        kept_stream = store_slot(kept_stream, clipped, stream_in, valid)
        kept_preact = store_slot(kept_preact, clipped, preact, valid)
        kept_hidden = store_slot(kept_hidden, clipped, hidden, valid)
        kept_grad = store_slot(
            kept_grad, clipped, cotangent, valid & (section_number == section_count - 1)
        )
        arrived = from_behind(result, "section", 1)
        return (arrived, kept_stream, kept_preact, kept_hidden, kept_grad)

    start = (
        jnp.zeros((micro_rows, feature_count), jnp.bfloat16),
        jnp.zeros((MICRO, micro_rows, feature_count), jnp.bfloat16),
        jnp.zeros((MICRO, micro_rows, hidden_count), jnp.float32),
        jnp.zeros((MICRO, micro_rows, hidden_count), jnp.bfloat16),
        jnp.zeros((MICRO, micro_rows, feature_count), jnp.bfloat16),
    )
    arrived, kept_stream, kept_preact, kept_hidden, kept_grad = lax.fori_loop(
        0, turn_count, forward_turn, start
    )

    def backward_turn(turn_index, carry):
        arrived_grad, kept_cotangent = carry
        micro_index = turn_index - (section_count - 1 - section_number)
        valid = (micro_index >= 0) & (micro_index < MICRO)
        clipped = jnp.clip(micro_index, 0, MICRO - 1)
        incoming = jnp.where(
            section_number == section_count - 1, pick_slot(kept_grad, clipped), arrived_grad
        )

        def backward_active(operand):
            return section_backward(
                incoming,
                pick_slot(kept_stream, clipped),
                pick_slot(scale_all, clipped),
                pick_slot(kept_preact, clipped),
                up_blocks,
                up_index,
                down_blocks,
                down_index,
            )

        def backward_resting(operand):
            return jnp.zeros_like(incoming)

        grad_stream = lax.cond(valid, backward_active, backward_resting, 0)
        kept_cotangent = store_slot(kept_cotangent, clipped, incoming, valid)
        arrived_grad = from_behind(grad_stream, "section", -1)
        return (arrived_grad, kept_cotangent)

    start_back = (
        jnp.zeros((micro_rows, feature_count), jnp.bfloat16),
        jnp.zeros((MICRO, micro_rows, feature_count), jnp.bfloat16),
    )
    arrived_grad, kept_cotangent = lax.fori_loop(0, turn_count, backward_turn, start_back)
    all_rows = MICRO * micro_rows
    hidden_rows = kept_hidden.reshape(all_rows, hidden_count)
    grad_rows_all = kept_cotangent.reshape(all_rows, feature_count)
    packed_rows = width_blocks * keep_down * block_size
    gathered = hidden_rows.reshape(all_rows, hidden_blocks, block_size)[:, down_index, :]
    weight_term = jnp.einsum(
        "tejh,tef->ejhf",
        gathered,
        grad_rows_all.reshape(all_rows, width_blocks, block_size),
        preferred_element_type=jnp.float32,
    )
    grad_down = lax.psum_scatter(
        weight_term.reshape(1, packed_rows, block_size), "dp", scatter_dimension=1, tiled=True
    )
    return grad_down


def solution(mesh):
    in_specs = (
        P("dp", None),
        P("dp", None),
        P("dp", None),
        P("dp"),
        P("section", None, None),
        P("section", "dp", None),
        P("section", None, None),
        P("section", None, None),
        P("section", None, None),
    )
    out_specs = P("section", "dp", None)
    return jax.shard_map(
        per_device, mesh=mesh, in_specs=in_specs, out_specs=out_specs, check_vma=False
    )
```

profile of v0, /device:TPU:4, one launch (start us, length us, event | category | flops | bytes accessed | tf_op | source)
XLA Modules:
  0.0 1123.6 jit_solution(2123157267478633781)
XLA Ops:
  16.2 81.9 %all-gather.2.cloned.1.call-done = bf16[1,36864,128]{2,1,0:T(8,128)(2,1)} async-done(((bf16[1,576,128]{2,1,0:T(8,128)(2,1)}), bf16[1,36864,128]{2,1,0:T(8,128)(2,1)}) %all-gather.2.cloned.1.call-update) | async-done | bytes 9437200 | tf_op jit(solution)/shard_map/all_gather | solution.py:113
  103.1 287.1 %while.39 = (s32[]{:T(128)}, bf16[64,1536]{1,0:T(8,128)(2,1)S(1)}, bf16[2,64,1536]{2,1,0:T(8,128)(2,1)}, f32[2,64,6144]{2,1,0:T(8,128)}, bf16[2,64,6144]{2,1,0:T...) while((s32[]{:T(128)}, bf16[64,1536]{1,0:T(8,128)(2,1)S(1)}, ...), condition=%wide.region_5.6_spmd, body=%wide.region_1.5_spmd.sunk | while | flops 1214156544 | bytes 98133112 | solution.py:169
  134.3 80.9 %collective-permute-done = bf16[64,1536]{1,0:T(8,128)(2,1)S(1)} collective-permute-done((bf16[64,1536]{1,0:T(8,128)(2,1)}, bf16[64,1536]{1,0:T(8,128)(2,1)S(1)}, u32[]{:S(2)}, u32[]{:S(2)}) %collective-permute-start) | collective-permute-done | bytes 196640 | tf_op jit(solution)/shard_map/while/body/eval_jaxpr/ppermute | solution.py:14
  217.8 45.3 %conditional.4 = (bf16[64,1536]{1,0:T(8,128)(2,1)S(1)}, f32[64,6144]{1,0:T(8,128)}, bf16[64,6144]{1,0:T(8,128)(2,1)S(1)}, f32[64,1536]{1,0:T(8,128)}) conditional(s32[]{:T(128)} %convert_element_type.162, () %tuple.92, (bf16[64,1536]{1,0:T(8,128)(2,1)S(1)}, f32[2,64,1536]{2,1,0:T(8,128)}, s32[]{:T(128)}, s32[48,6]{1,0:T(8,128)}, ...), branch_computations={%region_2.2_spmd, %region_3.4_spmd} | conditional | flops 1212681984 | bytes 56843296 | solution.py:148
  220.0 13.3 %gather_fusion = bf16[288,64,128]{2,1,0:T(8,128)(2,1)} fusion(bf16[64,12,128]{2,0,1:T(8,128)(2,1)S(1)} %copy_bitcast_fusion.2, s32[1024]{0:T(1024)S(1)} %pad_clamp_fusion.1), kind=kCustom, calls=%fused_computation | custom fusion | bytes 9438336 | tf_op jit(solution)/shard_map/while/body/eval_jaxpr/cond/branch_1_fun/gather | solution.py:34
  240.5 13.3 %gather_fusion.1 = bf16[288,64,128]{2,1,0:T(8,128)(2,1)} fusion(bf16[64,48,128]{2,0,1:T(8,128)(2,1)S(1)} %get-tuple-element.731, s32[1024]{0:T(1024)S(1)} %pad_clamp_fusion), kind=kCustom, calls=%fused_computation.1 | custom fusion | bytes 9438336 | tf_op jit(solution)/shard_map/while/body/eval_jaxpr/cond/branch_1_fun/gather | solution.py:37
  277.2 45.3 %conditional.4 = (bf16[64,1536]{1,0:T(8,128)(2,1)S(1)}, f32[64,6144]{1,0:T(8,128)}, bf16[64,6144]{1,0:T(8,128)(2,1)S(1)}, f32[64,1536]{1,0:T(8,128)}) conditional(s32[]{:T(128)} %convert_element_type.162, () %tuple.92, (bf16[64,1536]{1,0:T(8,128)(2,1)S(1)}, f32[2,64,1536]{2,1,0:T(8,128)}, s32[]{:T(128)}, s32[48,6]{1,0:T(8,128)}, ...), branch_computations={%region_2.2_spmd, %region_3.4_spmd} | conditional | flops 1212681984 | bytes 56843296 | solution.py:148
  279.4 13.3 %gather_fusion = bf16[288,64,128]{2,1,0:T(8,128)(2,1)} fusion(bf16[64,12,128]{2,0,1:T(8,128)(2,1)S(1)} %copy_bitcast_fusion.2, s32[1024]{0:T(1024)S(1)} %pad_clamp_fusion.1), kind=kCustom, calls=%fused_computation | custom fusion | bytes 9438336 | tf_op jit(solution)/shard_map/while/body/eval_jaxpr/cond/branch_1_fun/gather | solution.py:34
  299.9 13.3 %gather_fusion.1 = bf16[288,64,128]{2,1,0:T(8,128)(2,1)} fusion(bf16[64,48,128]{2,0,1:T(8,128)(2,1)S(1)} %get-tuple-element.731, s32[1024]{0:T(1024)S(1)} %pad_clamp_fusion), kind=kCustom, calls=%fused_computation.1 | custom fusion | bytes 9438336 | tf_op jit(solution)/shard_map/while/body/eval_jaxpr/cond/branch_1_fun/gather | solution.py:37
  339.5 42.7 %collective-permute-start = (bf16[64,1536]{1,0:T(8,128)(2,1)}, bf16[64,1536]{1,0:T(8,128)(2,1)S(1)}, u32[]{:S(2)}, u32[]{:S(2)}) collective-permute-start(bf16[64,1536]{1,0:T(8,128)(2,1)} %copy-done.6), channel_id=1, source_target_pairs={{0,64},{64,128},{128,192},{1,65},{65,129},{129,193},{2,66},{66,130... | collective-permute-start | bytes 589832 | tf_op jit(solution)/shard_map/while/body/eval_jaxpr/ppermute | solution.py:14
  391.0 407.0 %while.40 = (s32[]{:T(128)}, bf16[64,1536]{1,0:T(8,128)(2,1)S(1)}, bf16[2,64,1536]{2,1,0:T(8,128)(2,1)}, s32[]{:T(128)}, pred[]{:T(512)}, /*index=5*/bf16[2,64,1...) while((s32[]{:T(128)}, bf16[64,1536]{1,0:T(8,128)(2,1)S(1)}, ...), condition=%wide.region_13.14_spmd, body=%wide.region_6.13_spmd.sunk | while | flops 1222706944 | bytes 115030680 | solution.py:206
  396.3 92.5 %collective-permute-done.1 = bf16[64,1536]{1,0:T(8,128)(2,1)S(1)} collective-permute-done((bf16[64,1536]{1,0:T(8,128)(2,1)}, bf16[64,1536]{1,0:T(8,128)(2,1)S(1)}, u32[]{:S(2)}, u32[]{:S(2)}) %collective-permute-start.1) | collective-permute-done | bytes 196640 | tf_op jit(solution)/shard_map/while/body/eval_jaxpr/ppermute | solution.py:14
  491.4 89.1 %conditional.5 = (bf16[64,1536]{1,0:T(8,128)(2,1)S(1)}) conditional(s32[]{:T(128)} %convert_element_type.163, () %tuple.96, (bf16[64,1536]{1,0:T(8,128)(2,1)S(1)}, s32[]{:T(128)}, bf16[2,64,1536]{2,1,0:T(8,128)(2,1)}, s32[48,6]{1,0:T(8,128)}, s32[12,24]{1,0:T(8,128)S(1)}, /*index=5*/bf16[12,24,128,128]{3,2,1,0:T(8,128)(2,1)}, ...), branch_computations={%region_7.7_spmd, %region_8.12_spmd} | conditional | flops 1222510336 | bytes 112080184 | solution.py:197
  493.4 10.7 fusion.42
  504.4 29.7 %scatter_fusion = f32[64,48,128]{2,0,1:T(8,128)S(1)} fusion(f32[64,48,128]{2,0,1:T(8,128)S(1)} %broadcast.178, s32[288]{0:T(512)S(1)} %reshape.165, f32[288,64,128]{2,1,0:T(8,128)} %bitcast.172), kind=kCustom, calls=%fused_computation.3 | custom fusion | flops 2359296 | bytes 28312704 | tf_op jit(solution)/shard_map/while/body/eval_jaxpr/cond/branch_1_fun/scatter-add | solution.py:58
  545.8 29.9 %scatter_fusion.1 = f32[64,12,128]{2,0,1:T(8,128)S(1)} fusion(f32[64,12,128]{2,0,1:T(8,128)S(1)} %broadcast.175, s32[288]{0:T(512)S(1)} %reshape.173, f32[288,64,128]{2,1,0:T(8,128)} %bitcast.174), kind=kCustom, calls=%fused_computation.4 | custom fusion | flops 2359296 | bytes 28312704 | tf_op jit(solution)/shard_map/while/body/eval_jaxpr/cond/branch_1_fun/scatter-add | solution.py:70
  591.6 89.1 %conditional.5 = (bf16[64,1536]{1,0:T(8,128)(2,1)S(1)}) conditional(s32[]{:T(128)} %convert_element_type.163, () %tuple.96, (bf16[64,1536]{1,0:T(8,128)(2,1)S(1)}, s32[]{:T(128)}, bf16[2,64,1536]{2,1,0:T(8,128)(2,1)}, s32[48,6]{1,0:T(8,128)}, s32[12,24]{1,0:T(8,128)S(1)}, /*index=5*/bf16[12,24,128,128]{3,2,1,0:T(8,128)(2,1)}, ...), branch_computations={%region_7.7_spmd, %region_8.12_spmd} | conditional | flops 1222510336 | bytes 112080184 | solution.py:197
  593.6 10.7 fusion.42
  604.5 29.7 %scatter_fusion = f32[64,48,128]{2,0,1:T(8,128)S(1)} fusion(f32[64,48,128]{2,0,1:T(8,128)S(1)} %broadcast.178, s32[288]{0:T(512)S(1)} %reshape.165, f32[288,64,128]{2,1,0:T(8,128)} %bitcast.172), kind=kCustom, calls=%fused_computation.3 | custom fusion | flops 2359296 | bytes 28312704 | tf_op jit(solution)/shard_map/while/body/eval_jaxpr/cond/branch_1_fun/scatter-add | solution.py:58
  634.3 10.7 fusion.25
  645.9 29.9 %scatter_fusion.1 = f32[64,12,128]{2,0,1:T(8,128)S(1)} fusion(f32[64,12,128]{2,0,1:T(8,128)S(1)} %broadcast.175, s32[288]{0:T(512)S(1)} %reshape.173, f32[288,64,128]{2,1,0:T(8,128)} %bitcast.174), kind=kCustom, calls=%fused_computation.4 | custom fusion | flops 2359296 | bytes 28312704 | tf_op jit(solution)/shard_map/while/body/eval_jaxpr/cond/branch_1_fun/scatter-add | solution.py:70
  692.4 90.9 %collective-permute-start.1 = (bf16[64,1536]{1,0:T(8,128)(2,1)}, bf16[64,1536]{1,0:T(8,128)(2,1)S(1)}, u32[]{:S(2)}, u32[]{:S(2)}) collective-permute-start(bf16[64,1536]{1,0:T(8,128)(2,1)} %copy-done.7), channel_id=1, source_target_pairs={{64,0},{128,64},{192,128},{65,1},{129,65},{193,129},{66,2},{130,66... | collective-permute-start | bytes 589832 | tf_op jit(solution)/shard_map/while/body/eval_jaxpr/ppermute | solution.py:14
  812.0 12.7 %copy.62 = bf16[12,24,128,128]{2,3,1,0:T(8,128)(2,1)} copy(bf16[12,24,128,128]{3,2,1,0:T(8,128)(2,1)} %bitcast.180) | data formatting | bytes 18874368 | tf_op jit(solution)/shard_map/gather | solution.py:211
  834.9 281.8 %reduce-scatter.2.cloned.1.call-done = f32[1,576,128]{2,1,0:T(8,128)} async-done(((f32[1,36864,128]{2,1,0:T(8,128)}), f32[1,576,128]{2,1,0:T(8,128)}) %reduce-scatter.2.cloned.1.call-update) | async-done | bytes 294928 | tf_op jit(solution)/shard_map/reduce_scatter | solution.py:218
  (267 shorter events, 227.7 us)
Async XLA Ops:
  6.5 91.6 %all-gather.2.cloned.1.call-start = ((), (), s32[]{:S(2)}) async-start(), calls=%async_computation.1 | async-start | bytes 9584640 | tf_op jit(solution)/shard_map/all_gather | solution.py:113
  7.3 1109.5 %reduce-scatter.2.cloned.1.call-start = ((), (), s32[]{:S(2)}) async-start(), calls=%async_computation.2 | async-start | bytes 19169280 | tf_op jit(solution)/shard_map/reduce_scatter | solution.py:218
  108.6 10.3 collective-permute-start
  114.4 2.0 copy-start.1
  115.7 2.0 copy-start.4
  115.7 2.0 copy-start.8
  125.2 90.0 %collective-permute-start = (bf16[64,1536]{1,0:T(8,128)(2,1)}, bf16[64,1536]{1,0:T(8,128)(2,1)S(1)}, u32[]{:S(2)}, u32[]{:S(2)}) collective-permute-start(bf16[64,1536]{1,0:T(8,128)(2,1)} %copy-done.6), channel_id=1, source_target_pairs={{0,64},{64,128},{128,192},{1,65},{65,129},{129,193},{2,66},{66,130... | collective-permute-start | bytes 589832 | tf_op jit(solution)/shard_map/while/body/eval_jaxpr/ppermute | solution.py:14
  129.8 2.0 copy-start.1
  131.2 2.0 copy-start.4
  131.2 2.0 copy-start.8
  134.3 80.9 %copy-start.5 = (bf16[2,64,1536]{2,1,0:T(8,128)(2,1)}, bf16[2,64,1536]{2,1,0:T(8,128)(2,1)S(1)}, u32[]{:S(2)}) copy-start(bf16[2,64,1536]{2,1,0:T(8,128)(2,1)S(1)} %fusion.68) | copy-start | bytes 1179652 | tf_op jit(solution)/shard_map/while
  263.8 10.8 collective-permute-start
  268.4 2.9 copy-start.1
  323.2 10.0 collective-permute-start
  327.8 2.9 copy-start.1
  339.5 49.9 %collective-permute-start = (bf16[64,1536]{1,0:T(8,128)(2,1)}, bf16[64,1536]{1,0:T(8,128)(2,1)S(1)}, u32[]{:S(2)}, u32[]{:S(2)}) collective-permute-start(bf16[64,1536]{1,0:T(8,128)(2,1)} %copy-done.6), channel_id=1, source_target_pairs={{0,64},{64,128},{128,192},{1,65},{65,129},{129,193},{2,66},{66,130... | collective-permute-start | bytes 589832 | tf_op jit(solution)/shard_map/while/body/eval_jaxpr/ppermute | solution.py:14
  384.9 2.0 copy-start.1
  386.2 2.1 copy-start.4
  386.2 2.1 copy-start.8
  394.4 94.4 %collective-permute-start.1 = (bf16[64,1536]{1,0:T(8,128)(2,1)}, bf16[64,1536]{1,0:T(8,128)(2,1)S(1)}, u32[]{:S(2)}, u32[]{:S(2)}) collective-permute-start(bf16[64,1536]{1,0:T(8,128)(2,1)} %copy-done.7), channel_id=1, source_target_pairs={{64,0},{128,64},{192,128},{65,1},{129,65},{193,129},{66,2},{130,66... | collective-permute-start | bytes 589832 | tf_op jit(solution)/shard_map/while/body/eval_jaxpr/ppermute | solution.py:14
  581.2 7.8 collective-permute-start.1
  681.3 7.8 collective-permute-start.1
  692.4 94.4 %collective-permute-start.1 = (bf16[64,1536]{1,0:T(8,128)(2,1)}, bf16[64,1536]{1,0:T(8,128)(2,1)S(1)}, u32[]{:S(2)}, u32[]{:S(2)}) collective-permute-start(bf16[64,1536]{1,0:T(8,128)(2,1)} %copy-done.7), channel_id=1, source_target_pairs={{64,0},{128,64},{192,128},{65,1},{129,65},{193,129},{66,2},{130,66... | collective-permute-start | bytes 589832 | tf_op jit(solution)/shard_map/while/body/eval_jaxpr/ppermute | solution.py:14
  790.2 7.8 collective-permute-start.1
  (34 other events, 37.0 us)
Sparse Core Ops, SparseCore 0:
  10.1 87.9 all-gather.1
  835.1 281.6 reduce-scatter.1
where the time goes:
time: 1130 us; the launch traced here: 1120 us
  waiting for transfers between devices  557 us (49%)
  other arithmetic  176 us (16%)
  starting transfers between devices  152 us (13%)
  local copies, waits for them, and re-layouts  142 us (13%)
  matrix products  81.4 us (7%)
  between operations  13.5 us (1%)
    reduce_scatter x1, waiting for transfers between devices, per_device(): lax.psum_scatter(weight_term.reshape(1, packed_rows, block_size), 'dp', s...  282 us
    ppermute x10, waiting for transfers between devices, from_behind(): return lax.ppermute(block, axis, route)  193 us
    ppermute x10, starting transfers between devices, from_behind(): return lax.ppermute(block, axis, route)  152 us
    all_gather x1, waiting for transfers between devices, per_device(): gathered_up = lax.all_gather(up_weight, 'dp', axis=1, tiled=True)  81.9 us
    scatter-add x2, other arithmetic, section_backward(): grad_normed = jnp.zeros((row_count, feature_count // block_size, block_si...  59.7 us
    scatter-add x2, other arithmetic, section_backward(): grad_hidden = jnp.zeros((row_count, hidden_count // block_size, block_siz...  59.5 us
    dynamic_update_slice x25, other arithmetic, store_slot(): lax.dynamic_update_index_in_dim(stack, jnp.where(valid, value, previous),...  33 us
    gather x2, local copies, waits for them, and re-layouts, section_forward(): gathered = hidden[:, down_index, :]  26.7 us
  transfers between devices with their start and end apart: 12, of which 9 were waited for; matrix products, arithmetic and copies ran while one was open for 3% of the time, Pallas kernels for 0%

commit v1 on v0

--- a/solution.py
+++ b/solution.py
@@ -110,7 +110,12 @@
     micro_rows = row_total // MICRO
     turn_count = MICRO + section_count - 1
     loss_scale = 1.0 / math.sqrt(row_total * owner_count)
-    gathered_up = lax.all_gather(up_weight, "dp", axis=1, tiled=True)
+    gathered_up = jnp.concatenate(
+        jax.lax.all_to_all(
+            jnp.stack([up_weight for _ in range(jax.lax.psum(1, "dp"))], axis=0), "dp", 0, 0
+        ),
+        axis=1,
+    )
     up_blocks = gathered_up.reshape(hidden_blocks, keep_up, block_size, block_size)
     up_index = up_rows[0]
     down_blocks = down_weight.reshape(width_blocks, keep_down, block_size, block_size)

time: 1130 us -> 1270 us (1.12)
  waiting for transfers between devices: 557 us -> 679 us
  starting transfers between devices: 152 us -> 165 us
    all_to_all x0 -> x1, waiting for transfers between devices: none -> 204 us  [per_device(): jax.lax.all_to_all(jnp.stack([up_weight for _ in range(jax.lax.psum(1, 'd...]
    all_gather x1 -> x0, waiting for transfers between devices: 81.9 us -> none  [per_device(): gathered_up = lax.all_gather(up_weight, 'dp', axis=1, tiled=True)]
  transfers between devices with their start and end apart: 12 -> 12, of which waited for: 9 -> 9; matrix products, arithmetic and copies ran while one was open for 3% -> 2% of each run, Pallas kernels for 0% -> 0%
where the time goes in v1:
time: 1270 us; the launch traced here: 1260 us
  waiting for transfers between devices  679 us (53%)
  other arithmetic  172 us (14%)
  starting transfers between devices  165 us (13%)
  local copies, waits for them, and re-layouts  148 us (12%)
  matrix products  81.4 us (6%)
  between operations  13.5 us (1%)
    reduce_scatter x1, waiting for transfers between devices, per_device(): lax.psum_scatter(weight_term.reshape(1, packed_rows, block_size), 'dp', s...  282 us
    all_to_all x1, waiting for transfers between devices, per_device(): jax.lax.all_to_all(jnp.stack([up_weight for _ in range(jax.lax.psum(1, 'd...  204 us
    ppermute x10, waiting for transfers between devices, from_behind(): return lax.ppermute(block, axis, route)  194 us
    ppermute x10, starting transfers between devices, from_behind(): return lax.ppermute(block, axis, route)  153 us
    scatter-add x2, other arithmetic, section_backward(): grad_normed = jnp.zeros((row_count, feature_count // block_size, block_si...  59.7 us
    scatter-add x2, other arithmetic, section_backward(): grad_hidden = jnp.zeros((row_count, hidden_count // block_size, block_siz...  59.5 us
    dynamic_update_slice x25, other arithmetic, store_slot(): lax.dynamic_update_index_in_dim(stack, jnp.where(valid, value, previous),...  33.1 us
    gather x2, local copies, waits for them, and re-layouts, section_forward(): gathered = hidden[:, down_index, :]  26.7 us
  transfers between devices with their start and end apart: 12, of which 9 were waited for; matrix products, arithmetic and copies ran while one was open for 2% of the time, Pallas kernels for 0%

profile of v1, /device:TPU:4, one launch (start us, length us, event | category | flops | bytes accessed | tf_op | source)
XLA Modules:
  0.0 1259.8 jit_solution(2660246868386327079)
XLA Ops:
  13.4 12.5 all-to-all-start
  29.6 203.7 %all-to-all-done = bf16[64,1,576,128]{3,2,1,0:T(8,128)(2,1)} async-done(((bf16[64,1,576,128]{3,2,1,0:T(8,128)(2,1)}), bf16[64,1,576,128]{3,2,1,0:T(8,128)(2,1)}, u32[]{:S(2)}, u32[]{:S(2)}) %all-to-all-start) | async-done | bytes 9437216 | tf_op jit(solution)/shard_map/all_to_all | solution.py:114
  238.2 287.8 %while.39 = (s32[]{:T(128)}, bf16[64,1536]{1,0:T(8,128)(2,1)S(1)}, bf16[2,64,1536]{2,1,0:T(8,128)(2,1)}, f32[2,64,6144]{2,1,0:T(8,128)}, bf16[2,64,6144]{2,1,0:T...) while((s32[]{:T(128)}, bf16[64,1536]{1,0:T(8,128)(2,1)S(1)}, ...), condition=%wide.region_5.6_spmd, body=%wide.region_1.5_spmd.sunk | while | flops 1214156544 | bytes 98133112 | solution.py:174
  269.6 81.3 %collective-permute-done = bf16[64,1536]{1,0:T(8,128)(2,1)S(1)} collective-permute-done((bf16[64,1536]{1,0:T(8,128)(2,1)}, bf16[64,1536]{1,0:T(8,128)(2,1)S(1)}, u32[]{:S(2)}, u32[]{:S(2)}) %collective-permute-start) | collective-permute-done | bytes 196640 | tf_op jit(solution)/shard_map/while/body/eval_jaxpr/ppermute | solution.py:14
  353.6 45.3 %conditional.4 = (bf16[64,1536]{1,0:T(8,128)(2,1)S(1)}, f32[64,6144]{1,0:T(8,128)}, bf16[64,6144]{1,0:T(8,128)(2,1)S(1)}, f32[64,1536]{1,0:T(8,128)}) conditional(s32[]{:T(128)} %convert_element_type.162, () %tuple.92, (bf16[64,1536]{1,0:T(8,128)(2,1)S(1)}, f32[2,64,1536]{2,1,0:T(8,128)}, s32[]{:T(128)}, s32[48,6]{1,0:T(8,128)}, ...), branch_computations={%region_2.2_spmd, %region_3.4_spmd} | conditional | flops 1212681984 | bytes 56843296 | solution.py:153
  355.7 13.3 %gather_fusion = bf16[288,64,128]{2,1,0:T(8,128)(2,1)} fusion(bf16[64,12,128]{2,0,1:T(8,128)(2,1)S(1)} %copy_bitcast_fusion.2, s32[1024]{0:T(1024)S(1)} %pad_clamp_fusion.1), kind=kCustom, calls=%fused_computation | custom fusion | bytes 9438336 | tf_op jit(solution)/shard_map/while/body/eval_jaxpr/cond/branch_1_fun/gather | solution.py:34
  376.3 13.3 %gather_fusion.1 = bf16[288,64,128]{2,1,0:T(8,128)(2,1)} fusion(bf16[64,48,128]{2,0,1:T(8,128)(2,1)S(1)} %get-tuple-element.731, s32[1024]{0:T(1024)S(1)} %pad_clamp_fusion), kind=kCustom, calls=%fused_computation.1 | custom fusion | bytes 9438336 | tf_op jit(solution)/shard_map/while/body/eval_jaxpr/cond/branch_1_fun/gather | solution.py:37
  412.9 45.2 %conditional.4 = (bf16[64,1536]{1,0:T(8,128)(2,1)S(1)}, f32[64,6144]{1,0:T(8,128)}, bf16[64,6144]{1,0:T(8,128)(2,1)S(1)}, f32[64,1536]{1,0:T(8,128)}) conditional(s32[]{:T(128)} %convert_element_type.162, () %tuple.92, (bf16[64,1536]{1,0:T(8,128)(2,1)S(1)}, f32[2,64,1536]{2,1,0:T(8,128)}, s32[]{:T(128)}, s32[48,6]{1,0:T(8,128)}, ...), branch_computations={%region_2.2_spmd, %region_3.4_spmd} | conditional | flops 1212681984 | bytes 56843296 | solution.py:153
  415.1 13.3 %gather_fusion = bf16[288,64,128]{2,1,0:T(8,128)(2,1)} fusion(bf16[64,12,128]{2,0,1:T(8,128)(2,1)S(1)} %copy_bitcast_fusion.2, s32[1024]{0:T(1024)S(1)} %pad_clamp_fusion.1), kind=kCustom, calls=%fused_computation | custom fusion | bytes 9438336 | tf_op jit(solution)/shard_map/while/body/eval_jaxpr/cond/branch_1_fun/gather | solution.py:34
  435.6 13.3 %gather_fusion.1 = bf16[288,64,128]{2,1,0:T(8,128)(2,1)} fusion(bf16[64,48,128]{2,0,1:T(8,128)(2,1)S(1)} %get-tuple-element.731, s32[1024]{0:T(1024)S(1)} %pad_clamp_fusion), kind=kCustom, calls=%fused_computation.1 | custom fusion | bytes 9438336 | tf_op jit(solution)/shard_map/while/body/eval_jaxpr/cond/branch_1_fun/gather | solution.py:37
  475.1 43.0 %collective-permute-start = (bf16[64,1536]{1,0:T(8,128)(2,1)}, bf16[64,1536]{1,0:T(8,128)(2,1)S(1)}, u32[]{:S(2)}, u32[]{:S(2)}) collective-permute-start(bf16[64,1536]{1,0:T(8,128)(2,1)} %copy-done.6), channel_id=1, source_target_pairs={{0,64},{64,128},{128,192},{1,65},{65,129},{129,193},{2,66},{66,130... | collective-permute-start | bytes 589832 | tf_op jit(solution)/shard_map/while/body/eval_jaxpr/ppermute | solution.py:14
  526.9 407.3 %while.40 = (s32[]{:T(128)}, bf16[64,1536]{1,0:T(8,128)(2,1)S(1)}, bf16[2,64,1536]{2,1,0:T(8,128)(2,1)}, s32[]{:T(128)}, pred[]{:T(512)}, /*index=5*/bf16[2,64,1...) while((s32[]{:T(128)}, bf16[64,1536]{1,0:T(8,128)(2,1)S(1)}, ...), condition=%wide.region_13.14_spmd, body=%wide.region_6.13_spmd.sunk | while | flops 1222706944 | bytes 115030680 | solution.py:211
  532.1 92.9 %collective-permute-done.1 = bf16[64,1536]{1,0:T(8,128)(2,1)S(1)} collective-permute-done((bf16[64,1536]{1,0:T(8,128)(2,1)}, bf16[64,1536]{1,0:T(8,128)(2,1)S(1)}, u32[]{:S(2)}, u32[]{:S(2)}) %collective-permute-start.1) | collective-permute-done | bytes 196640 | tf_op jit(solution)/shard_map/while/body/eval_jaxpr/ppermute | solution.py:14
  627.6 89.0 %conditional.5 = (bf16[64,1536]{1,0:T(8,128)(2,1)S(1)}) conditional(s32[]{:T(128)} %convert_element_type.163, () %tuple.96, (bf16[64,1536]{1,0:T(8,128)(2,1)S(1)}, s32[]{:T(128)}, bf16[2,64,1536]{2,1,0:T(8,128)(2,1)}, s32[48,6]{1,0:T(8,128)}, s32[12,24]{1,0:T(8,128)S(1)}, /*index=5*/bf16[12,24,128,128]{3,2,1,0:T(8,128)(2,1)}, ...), branch_computations={%region_7.7_spmd, %region_8.12_spmd} | conditional | flops 1222510336 | bytes 112080184 | solution.py:202
  629.6 10.7 fusion.42
  640.6 29.7 %scatter_fusion = f32[64,48,128]{2,0,1:T(8,128)S(1)} fusion(f32[64,48,128]{2,0,1:T(8,128)S(1)} %broadcast.181, s32[288]{0:T(512)S(1)} %reshape.164, f32[288,64,128]{2,1,0:T(8,128)} %bitcast.173), kind=kCustom, calls=%fused_computation.3 | custom fusion | flops 2359296 | bytes 28312704 | tf_op jit(solution)/shard_map/while/body/eval_jaxpr/cond/branch_1_fun/scatter-add | solution.py:58
  681.9 29.9 %scatter_fusion.1 = f32[64,12,128]{2,0,1:T(8,128)S(1)} fusion(f32[64,12,128]{2,0,1:T(8,128)S(1)} %broadcast.178, s32[288]{0:T(512)S(1)} %reshape.172, f32[288,64,128]{2,1,0:T(8,128)} %bitcast.174), kind=kCustom, calls=%fused_computation.4 | custom fusion | flops 2359296 | bytes 28312704 | tf_op jit(solution)/shard_map/while/body/eval_jaxpr/cond/branch_1_fun/scatter-add | solution.py:70
  727.8 89.1 %conditional.5 = (bf16[64,1536]{1,0:T(8,128)(2,1)S(1)}) conditional(s32[]{:T(128)} %convert_element_type.163, () %tuple.96, (bf16[64,1536]{1,0:T(8,128)(2,1)S(1)}, s32[]{:T(128)}, bf16[2,64,1536]{2,1,0:T(8,128)(2,1)}, s32[48,6]{1,0:T(8,128)}, s32[12,24]{1,0:T(8,128)S(1)}, /*index=5*/bf16[12,24,128,128]{3,2,1,0:T(8,128)(2,1)}, ...), branch_computations={%region_7.7_spmd, %region_8.12_spmd} | conditional | flops 1222510336 | bytes 112080184 | solution.py:202
  729.7 10.7 fusion.42
  740.7 29.7 %scatter_fusion = f32[64,48,128]{2,0,1:T(8,128)S(1)} fusion(f32[64,48,128]{2,0,1:T(8,128)S(1)} %broadcast.181, s32[288]{0:T(512)S(1)} %reshape.164, f32[288,64,128]{2,1,0:T(8,128)} %bitcast.173), kind=kCustom, calls=%fused_computation.3 | custom fusion | flops 2359296 | bytes 28312704 | tf_op jit(solution)/shard_map/while/body/eval_jaxpr/cond/branch_1_fun/scatter-add | solution.py:58
  782.1 29.9 %scatter_fusion.1 = f32[64,12,128]{2,0,1:T(8,128)S(1)} fusion(f32[64,12,128]{2,0,1:T(8,128)S(1)} %broadcast.178, s32[288]{0:T(512)S(1)} %reshape.172, f32[288,64,128]{2,1,0:T(8,128)} %bitcast.174), kind=kCustom, calls=%fused_computation.4 | custom fusion | flops 2359296 | bytes 28312704 | tf_op jit(solution)/shard_map/while/body/eval_jaxpr/cond/branch_1_fun/scatter-add | solution.py:70
  828.6 90.9 %collective-permute-start.1 = (bf16[64,1536]{1,0:T(8,128)(2,1)}, bf16[64,1536]{1,0:T(8,128)(2,1)S(1)}, u32[]{:S(2)}, u32[]{:S(2)}) collective-permute-start(bf16[64,1536]{1,0:T(8,128)(2,1)} %copy-done.7), channel_id=1, source_target_pairs={{64,0},{128,64},{192,128},{65,1},{129,65},{193,129},{66,2},{130,66... | collective-permute-start | bytes 589832 | tf_op jit(solution)/shard_map/while/body/eval_jaxpr/ppermute | solution.py:14
  948.2 12.7 %copy.79 = bf16[12,24,128,128]{2,3,1,0:T(8,128)(2,1)} copy(bf16[12,24,128,128]{3,2,1,0:T(8,128)(2,1)} %bitcast.180) | data formatting | bytes 18874368 | tf_op jit(solution)/shard_map/gather | solution.py:216
  971.1 281.8 %reduce-scatter.2.cloned.1.call-done = f32[1,576,128]{2,1,0:T(8,128)} async-done(((f32[1,36864,128]{2,1,0:T(8,128)}), f32[1,576,128]{2,1,0:T(8,128)}) %reduce-scatter.2.cloned.1.call-update) | async-done | bytes 294928 | tf_op jit(solution)/shard_map/reduce_scatter | solution.py:223
  (279 shorter events, 238.8 us)
Async XLA Ops:
  13.4 12.6 copy-start.14
  13.4 13.3 %copy-start.13 = (s32[1,12,24]{2,0,1:T(1,128)S(1)}, s32[1,12,24]{2,0,1:T(1,128)}, u32[]{:S(2)}) copy-start(s32[1,12,24]{2,0,1:T(1,128)} %param.25) | copy-start | bytes 3460
  13.4 14.0 %copy-start.15 = (s32[128]{0:T(128)S(1)}, s32[128]{0:T(128)}, u32[]{:S(2)}) copy-start(s32[128]{0:T(128)} %param.20) | copy-start | bytes 1540
  13.4 14.0 %copy-start.12 = (f32[1,4,1536]{2,1,0:T(4,128)S(1)}, f32[1,4,1536]{2,1,0:T(4,128)}, u32[]{:S(2)}) copy-start(f32[1,4,1536]{2,1,0:T(4,128)} %param.21) | copy-start | bytes 73732
  13.4 15.2 %copy-start.9 = (bf16[128,1536]{1,0:T(8,128)(2,1)S(1)}, bf16[128,1536]{1,0:T(8,128)(2,1)}, u32[]{:S(2)}) copy-start(bf16[128,1536]{1,0:T(8,128)(2,1)} %param.18) | copy-start | bytes 1179652
  13.4 15.2 %copy-start.10 = (bf16[128,1536]{1,0:T(8,128)(2,1)S(1)}, bf16[128,1536]{1,0:T(8,128)(2,1)}, u32[]{:S(2)}) copy-start(bf16[128,1536]{1,0:T(8,128)(2,1)} %param.17) | copy-start | bytes 1179652
  13.4 219.8 %all-to-all-start = ((bf16[64,1,576,128]{3,2,1,0:T(8,128)(2,1)}), bf16[64,1,576,128]{3,2,1,0:T(8,128)(2,1)}, u32[]{:S(2)}, u32[]{:S(2)}) async-start(bf16[64,1,576,128]{3,2,1,0:T(8,128)(2,1)} %stack.2), calls=%async_computation | async-start | bytes 18874368 | tf_op jit(solution)/shard_map/all_to_all | solution.py:114
  25.9 1227.0 %reduce-scatter.2.cloned.1.call-start = ((), (), s32[]{:S(2)}) async-start(), calls=%async_computation.2 | async-start | bytes 19169280 | tf_op jit(solution)/shard_map/reduce_scatter | solution.py:223
  243.9 10.3 collective-permute-start
  251.1 2.0 copy-start.8
  260.4 90.5 %collective-permute-start = (bf16[64,1536]{1,0:T(8,128)(2,1)}, bf16[64,1536]{1,0:T(8,128)(2,1)S(1)}, u32[]{:S(2)}, u32[]{:S(2)}) collective-permute-start(bf16[64,1536]{1,0:T(8,128)(2,1)} %copy-done.6), channel_id=1, source_target_pairs={{0,64},{64,128},{128,192},{1,65},{65,129},{129,193},{2,66},{66,130... | collective-permute-start | bytes 589832 | tf_op jit(solution)/shard_map/while/body/eval_jaxpr/ppermute | solution.py:14
  269.6 81.3 %copy-start.5 = (bf16[2,64,1536]{2,1,0:T(8,128)(2,1)}, bf16[2,64,1536]{2,1,0:T(8,128)(2,1)S(1)}, u32[]{:S(2)}) copy-start(bf16[2,64,1536]{2,1,0:T(8,128)(2,1)S(1)} %fusion.68) | copy-start | bytes 1179652 | tf_op jit(solution)/shard_map/while
  399.5 10.8 collective-permute-start
  404.1 2.9 copy-start.1
  458.8 10.0 collective-permute-start
  463.5 2.9 copy-start.1
  475.1 50.2 %collective-permute-start = (bf16[64,1536]{1,0:T(8,128)(2,1)}, bf16[64,1536]{1,0:T(8,128)(2,1)S(1)}, u32[]{:S(2)}, u32[]{:S(2)}) collective-permute-start(bf16[64,1536]{1,0:T(8,128)(2,1)} %copy-done.6), channel_id=1, source_target_pairs={{0,64},{64,128},{128,192},{1,65},{65,129},{129,193},{2,66},{66,130... | collective-permute-start | bytes 589832 | tf_op jit(solution)/shard_map/while/body/eval_jaxpr/ppermute | solution.py:14
  522.2 2.1 copy-start.4
  522.2 2.1 copy-start.8
  530.2 94.8 %collective-permute-start.1 = (bf16[64,1536]{1,0:T(8,128)(2,1)}, bf16[64,1536]{1,0:T(8,128)(2,1)S(1)}, u32[]{:S(2)}, u32[]{:S(2)}) collective-permute-start(bf16[64,1536]{1,0:T(8,128)(2,1)} %copy-done.7), channel_id=1, source_target_pairs={{64,0},{128,64},{192,128},{65,1},{129,65},{193,129},{66,2},{130,66... | collective-permute-start | bytes 589832 | tf_op jit(solution)/shard_map/while/body/eval_jaxpr/ppermute | solution.py:14
  717.4 7.8 collective-permute-start.1
  817.5 7.8 collective-permute-start.1
  828.6 94.4 %collective-permute-start.1 = (bf16[64,1536]{1,0:T(8,128)(2,1)}, bf16[64,1536]{1,0:T(8,128)(2,1)S(1)}, u32[]{:S(2)}, u32[]{:S(2)}) collective-permute-start(bf16[64,1536]{1,0:T(8,128)(2,1)} %copy-done.7), channel_id=1, source_target_pairs={{64,0},{128,64},{192,128},{65,1},{129,65},{193,129},{66,2},{130,66... | collective-permute-start | bytes 589832 | tf_op jit(solution)/shard_map/while/body/eval_jaxpr/ppermute | solution.py:14
  926.4 7.8 collective-permute-start.1
  (40 other events, 49.0 us)
Sparse Core Ops, SparseCore 0:
  971.2 281.6 reduce-scatter.1
